TPU v7x, 128 devices: a whole 4x4x4 slice. The times are simulated.
128 devices in a mesh: row: 16 (over x_hi, y, core), proto: 8 (over z, x_lo).
Axes of the slice: x: 4 (x_hi: 2, x_lo: 2; x = x_hi * 2 + x_lo), y: 4, z: 4, core: 2. Of those that a mesh axis runs over, the one named last changes fastest.
Arguments:
- tokens: bfloat16 [8192, 4096], P('row'), may hold values from -6 to 6
- w_in: bfloat16 [4096, 8192], P('row', 'proto'), may hold values from -0.09375 to 0.09375
- w_out: bfloat16 [8192, 384], P('proto'), may hold values from -0.0625 to 0.0625
- teacher_z: bfloat16 [8192, 384], P(('row', 'proto')), may hold values from -6 to 6
- proto_student: bfloat16 [384, 49152], P(None, 'proto'), may hold values from -48 to 48
- proto_teacher: bfloat16 [384, 49152], P(None, 'proto'), may hold values from -48 to 48
- center: float32 [49152], P('proto'), may hold values from -0.6 to 0.6
- image_of: int32 [8192], P('row'), may hold values from 0 to 63
Outputs:
- loss: float32 [], replicated
- w_in_grad: float32 [4096, 8192], P('row', 'proto')
- w_out_grad: float32 [8192, 384], P('proto')
- proto_grad: float32 [384, 49152], P('row', 'proto')
All inputs are finite; a program needn't handle non-finite values.
Results may differ from a plain program's by a relative error of at most 0.015.
Values may be sent and summed in bfloat16 or wider, within the bound.
A program may use at most 128 MiB of HBM per device.

v0:
```python
import jax
import jax.numpy as jnp
from jax import lax
from jax.sharding import PartitionSpec as P

tau_teacher = 0.07
tau_student = 0.1
loss_scale = 1048576.0
norm_eps = 1e-06


def gelu_parts(values):
    cumul = 0.5 * (1.0 + jax.scipy.special.erf(values * 0.7071067811865476))
    density = jnp.exp(-0.5 * values * values) * 0.3989422804014327
    return (values * cumul, cumul + values * density)


def inner(left, right):
    return lax.dot_general(
        left, right, (((0,), (0,)), ((), ())), preferred_element_type=jnp.float32
    )


def outer_last(left, right):
    return lax.dot_general(
        left, right, (((1,), (1,)), ((), ())), preferred_element_type=jnp.float32
    )


def normalize(values):
    recip = lax.rsqrt(jnp.sum(values * values, axis=1, keepdims=True) + norm_eps)
    return (recip, values * recip)


def teacher_norm(teacher_z):
    teach = teacher_z.astype(jnp.float32)
    return (teach * lax.rsqrt(jnp.sum(teach * teach, axis=1, keepdims=True) + norm_eps)).astype(
        jnp.bfloat16
    )


def back_norm(dnorm, recip, unit):
    return (recip * (dnorm - unit * jnp.sum(unit * dnorm, axis=1, keepdims=True))).astype(
        jnp.bfloat16
    )


def on_device(tokens, w_in, w_out, teacher_z, proto_student, proto_teacher, center, image_of):
    row_count = tokens.shape[0]
    images = row_count * lax.axis_size("row") // 128
    onehot = (image_of[:, None] == jnp.arange(images, dtype=jnp.int32)[None, :]).astype(jnp.float32)
    counts = lax.psum(jnp.sum(onehot, axis=0), "row")
    weight = 1.0 / (images * jnp.sum(onehot * counts[None, :], axis=1))
    pre = jnp.dot(
        tokens, lax.all_gather(w_in, "row", axis=0, tiled=True), preferred_element_type=jnp.float32
    )
    act, slope = gelu_parts(pre)
    hidden = act.astype(jnp.bfloat16)
    partial_value = jnp.dot(hidden, w_out, preferred_element_type=jnp.float32)
    bott = lax.psum(partial_value, "proto")
    recip, unit = normalize(bott)
    student_n = unit.astype(jnp.bfloat16)
    teacher_n = lax.all_gather(teacher_norm(teacher_z), "proto", axis=0, tiled=True)
    logit_t = (
        jnp.dot(teacher_n, proto_teacher, preferred_element_type=jnp.float32) - center[None, :]
    ) / tau_teacher
    logit_s = jnp.dot(student_n, proto_student, preferred_element_type=jnp.float32) / tau_student
    local_t = jnp.max(logit_t, axis=1)
    local_s = jnp.max(logit_s, axis=1)
    top_t, top_s = lax.pmax((local_t, local_s), "proto")
    exp_t = jnp.exp(logit_t - top_t[:, None])
    exp_s = jnp.exp(logit_s - top_s[:, None])
    total_t, total_s = lax.psum((jnp.sum(exp_t, axis=1), jnp.sum(exp_s, axis=1)), "proto")
    prob_t = exp_t / total_t[:, None]
    prob_s = exp_s / total_s[:, None]
    logp_s = logit_s - top_s[:, None] - jnp.log(total_s)[:, None]
    cross = -jnp.sum(prob_t * logp_s, axis=1)
    loss = lax.psum(jnp.sum(weight * cross), ("row", "proto"))
    grad_s = (loss_scale * weight[:, None] * (prob_s - prob_t) / tau_student).astype(jnp.bfloat16)
    proto_grad = lax.psum_scatter(
        inner(student_n, grad_s).astype(jnp.bfloat16), "row", scatter_dimension=0, tiled=True
    ).astype(jnp.float32)
    dnorm_part = outer_last(grad_s, proto_student)
    dnorm = lax.psum(dnorm_part, "proto")
    dbott = back_norm(dnorm, recip, unit)
    w_out_grad = lax.psum(inner(hidden, dbott).astype(jnp.bfloat16), "row").astype(jnp.float32)
    dpre = (outer_last(dbott, w_out) * slope).astype(jnp.bfloat16)
    w_in_grad = lax.psum_scatter(
        inner(tokens, dpre).astype(jnp.bfloat16), "row", scatter_dimension=0, tiled=True
    ).astype(jnp.float32)
    return (loss, w_in_grad, w_out_grad, proto_grad)


def solution(mesh):
    return jax.shard_map(
        on_device,
        mesh=mesh,
        in_specs=(
            P("row", None),
            P("row", "proto"),
            P("proto", None),
            P(("row", "proto"), None),
            P(None, "proto"),
            P(None, "proto"),
            P("proto"),
            P("row"),
        ),
        out_specs=(P(), P("row", "proto"), P("proto", None), P("row", "proto")),
        check_vma=False,
    )
```

profile of v0, /device:TPU:0, one launch (start us, length us, event | category | flops | bytes accessed | tf_op | source)
XLA Modules:
  0.0 676.0 jit_solution(12270464372114535581)
XLA Ops:
  7.2 0.0 copy-start
  7.2 0.0 all-gather.2.cloned.1.call-start
  7.2 0.7 all-gather.2.cloned.1.call-update
  7.9 0.0 all-reduce.6.cloned.1.call-start
  8.0 0.8 convert_reduce_fusion
  8.8 38.4 %psum.49 = f32[64]{0:T(128)S(1)} all-reduce(f32[64]{0:T(128)S(1)} %convert_reduce_fusion), channel_id=1, replica_groups=mesh['row'=16,'proto'=8] {'row'}, use_global_device_ids=true, to_apply=%region_1.0 | all-reduce | flops 64 | bytes 512 | tf_op jit(solution)/shard_map/psum | solution.py:52
  47.2 0.9 fusion.9
  48.1 0.8 select_reduce_fusion
  48.9 0.9 fusion.10
  49.8 0.0 copy-start.3
  49.8 35.8 %all-gather.2.cloned.1.call-done = bf16[4096,1024]{1,0:T(8,128)(2,1)} async-done(((bf16[256,1024]{1,0:T(8,128)(2,1)}), bf16[4096,1024]{1,0:T(8,128)(2,1)}) %all-gather.2.cloned.1.call-update) | async-done | bytes 8388624 | tf_op jit(solution)/shard_map/all_gather | solution.py:55
  85.6 10.6 %multiply_convert_fusion.1 = (bf16[512,1024]{1,0:T(8,128)(2,1)S(1)}, f32[512,1024]{1,0:T(8,128)}) fusion(bf16[512,4096]{1,0:T(8,128)(2,1)} %param.8, bf16[4096,1024]{1,0:T(8,128)(2,1)} %all-gather.2.cloned.1.call-done), kind=kOutput, calls=%fused_computation.19 | convolution fusion | flops 4297588736 | bytes 15728640 | tf_op jit(solution)/shard_map/dot_general | solution.py:54
  96.2 1.6 fusion.14
  97.8 0.0 all-reduce.6.cloned.1.call-update
  97.8 0.0 all-reduce.8.cloned.1.call-start
  97.8 31.3 %all_gather.6 = bf16[512,384]{1,0:T(8,128)(2,1)S(1)} all-gather(bf16[64,384]{1,0:T(8,128)(2,1)S(1)} %fusion.10), channel_id=1, replica_groups=mesh['row'=16,'proto'=8] {'proto'}, dimensions={0}, use_global_device_ids=true | all-gather | bytes 442368 | tf_op jit(solution)/shard_map/all_gather | solution.py:63
  129.1 9.0 %fusion = (f32[512]{0:T(512)S(1)}, f32[512,6144]{1,0:T(8,128)}) fusion(f32[6144]{0:T(1024)S(1)} %copy-done.3, bf16[512,384]{1,0:T(8,128)(2,1)S(1)} %all_gather.6, bf16[384,6144]{1,0:T(8,128)(2,1)} %param.13), kind=kOutput, calls=%fused_computation.7 | convolution fusion | flops 2425355776 | bytes 17721344 | tf_op jit(solution)/shard_map/dot_general | solution.py:65
  138.2 37.0 %all-reduce.6.cloned.1.call-done = f32[512,384]{1,0:T(8,128)} async-done(((f32[512,384]{1,0:T(8,128)}), f32[512,384]{1,0:T(8,128)}) %all-reduce.6.cloned.1.call-update) | async-done | bytes 786448 | tf_op jit(solution)/shard_map/psum | solution.py:60
  175.2 1.3 multiply_reduce_fusion.3
  176.5 10.6 %multiply_reduce_fusion.1 = (f32[512]{0:T(512)S(1)}, f32[512,6144]{1,0:T(8,128)}) fusion(bf16[384,6144]{1,0:T(8,128)(2,1)} %param.12, f32[512,384]{1,0:T(8,128)} %all-reduce.6.cloned.1.call-done, f32[512]{0:T(512)S(1)} %add_rsqrt_fusion), kind=kOutput, calls=%fused_computation.6 | convolution fusion | flops 2422603264 | bytes 18092032 | tf_op jit(solution)/shard_map/dot_general | solution.py:67
  187.1 17.9 %all-reduce.1 = (f32[512]{0:T(512)S(1)}, f32[512]{0:T(512)S(1)}) all-reduce(f32[512]{0:T(512)S(1)} %get-tuple-element.20, f32[512]{0:T(512)S(1)} %get-tuple-element.22), channel_id=1, replica_groups=mesh['row'=16,'proto'=8] {'proto'}, use_global_device_ids=true, to_apply=%region_11.0 | all-reduce | flops 1024 | bytes 8192 | tf_op jit(solution)/shard_map/pmax | solution.py:70
  205.0 10.3 %exponential_reduce_fusion = (f32[512]{0:T(512)S(1)}, f32[512]{0:T(512)S(1)}) fusion(f32[512,6144]{1,0:T(8,128)} %get-tuple-element.21, f32[512]{0:T(512)S(1)} %get-tuple-element.14, f32[512]{0:T(512)S(1)} %get-tuple-element.15, f32[512,6144]{1,0:T(8,128)} %get-tuple-element.23, f32[6144]{0:T(1024)S(1)} %copy-done.3), kind=kLoop, calls=%fused_computation.4 | loop fusion | flops 22019072 | bytes 25198592 | tf_op jit(solution)/shard_map/reduce_sum | solution.py:73
  215.3 16.4 %all-reduce = (f32[512]{0:T(512)S(1)}, f32[512]{0:T(512)S(1)}) all-reduce(f32[512]{0:T(512)S(1)} %get-tuple-element.24, f32[512]{0:T(512)S(1)} %get-tuple-element.25), channel_id=1, replica_groups=mesh['row'=16,'proto'=8] {'proto'}, use_global_device_ids=true, to_apply=%region_13.0 | all-reduce | flops 1024 | bytes 8192 | tf_op jit(solution)/shard_map/psum | solution.py:73
  231.7 12.0 %multiply_convert_fusion = (bf16[512,6144]{1,0:T(8,128)(2,1)S(1)}, f32[512]{0:T(512)S(1)}) fusion(f32[512,6144]{1,0:T(8,128)} %get-tuple-element.21, f32[512]{0:T(512)S(1)} %get-tuple-element.12, f32[512]{0:T(512)S(1)} %broadcast_multiply_fusion, f32[512]{0:T(512)S(1)} %get-tuple-element.14, f32[512]{0:T(512)S(1)} %get-tuple-element.13, ...), kind=kLoop, calls=%fused_computation | loop fusion | flops 44039680 | bytes 31496192 | tf_op jit(solution)/shard_map/convert_element_type | solution.py:79
  243.7 0.0 copy-start.1
  243.7 2.7 copy-done.1
  246.3 6.7 fusion.15
  253.0 0.0 all-reduce.8.cloned.1.call-update
  253.0 0.0 all-reduce.10.cloned.1.call-start
  253.1 76.8 %all-reduce.8.cloned.1.call-done = f32[512,384]{1,0:T(8,128)} async-done(((f32[512,384]{1,0:T(8,128)}), f32[512,384]{1,0:T(8,128)}) %all-reduce.8.cloned.1.call-update) | async-done | bytes 786448 | tf_op jit(solution)/shard_map/psum | solution.py:84
  329.9 1.4 multiply_reduce_fusion.2
  331.3 1.3 multiply_convert_fusion.2
  332.6 1.7 convolution_convert_fusion.1
  334.3 0.0 all-reduce.10.cloned.1.call-update
  334.3 0.0 reduce-scatter.5.cloned.1.call-start
  334.4 7.7 %convolution_convert_fusion = bf16[384,6144]{1,0:T(8,128)(2,1)} fusion(bf16[512,6144]{1,0:T(8,128)(2,1)} %copy-done.1, f32[512,384]{1,0:T(8,128)S(1)} %copy-done.2, f32[512]{0:T(512)S(1)} %add_rsqrt_fusion), kind=kOutput, calls=%fused_computation.10 | convolution fusion | flops 2418671616 | bytes 11798528 | tf_op jit(solution)/shard_map/dot_general | solution.py:19
  342.0 0.0 reduce-scatter.5.cloned.1.call-update
  342.1 0.0 reduce-scatter.3.cloned.1.call-start
  342.1 10.4 %convert_bitcast_fusion = bf16[4096,1024]{0,1:T(8,128)(2,1)} fusion(bf16[512,4096]{1,0:T(8,128)(2,1)} %param.8, f32[512,1024]{1,0:T(8,128)} %get-tuple-element.19, bf16[512,384]{1,0:T(8,128)(2,1)S(1)} %multiply_convert_fusion.2, bf16[1024,384]{1,0:T(8,128)(2,1)S(1)} %copy-done), kind=kOutput, calls=%fused_computation.11 | convolution fusion | flops 4707057664 | bytes 15859712 | tf_op jit(solution)/shard_map/dot_general | solution.py:19
  352.5 0.0 reduce-scatter.3.cloned.1.call-update
  352.5 0.6 multiply_reduce_fusion.4
  353.1 63.4 %psum.53 = f32[]{:T(128)} all-reduce(f32[]{:T(128)} %multiply_reduce_fusion.4), channel_id=1, replica_groups=mesh['row'=16,'proto'=8] {'row','proto'}, use_global_device_ids=true, to_apply=%region_16.0 | all-reduce | flops 1 | bytes 8 | tf_op jit(solution)/shard_map/psum | solution.py:78
  416.5 57.5 %all-reduce.10.cloned.1.call-done = bf16[1024,384]{1,0:T(8,128)(2,1)} async-done(((bf16[1024,384]{1,0:T(8,128)(2,1)}), bf16[1024,384]{1,0:T(8,128)(2,1)}) %all-reduce.10.cloned.1.call-update) | async-done | bytes 786448 | tf_op jit(solution)/shard_map/psum | solution.py:86
  474.0 2.4 convert_element_type.57
  476.4 85.6 %reduce-scatter.5.cloned.1.call-done = bf16[24,6144]{1,0:T(8,128)(2,1)} async-done(((bf16[384,6144]{1,0:T(8,128)(2,1)}), bf16[24,6144]{1,0:T(8,128)(2,1)}) %reduce-scatter.5.cloned.1.call-update) | async-done | bytes 294928 | tf_op jit(solution)/shard_map/reduce_scatter | solution.py:80
  561.9 1.8 convert_element_type.59
  563.7 103.1 %reduce-scatter.3.cloned.1.call-done = bf16[256,1024]{0,1:T(8,128)(2,1)} async-done(((bf16[4096,1024]{0,1:T(8,128)(2,1)}), bf16[256,1024]{0,1:T(8,128)(2,1)}) %reduce-scatter.3.cloned.1.call-update) | async-done | bytes 524304 | tf_op jit(solution)/shard_map/reduce_scatter | solution.py:88
  666.9 2.2 copy.13
  (8 shorter events, 0.0 us)
Async XLA Ops:
  7.2 89.0 %copy-start = (bf16[1024,384]{1,0:T(8,128)(2,1)S(1)}, bf16[1024,384]{1,0:T(8,128)(2,1)}, u32[]{:S(2)}) copy-start(bf16[1024,384]{1,0:T(8,128)(2,1)} %param.10) | copy-start | bytes 2359300
  7.2 78.4 %all-gather.2.cloned.1.call-start = ((), (), s32[]{:S(2)}) async-start(), calls=%async_computation.2 | async-start | bytes 8912896 | tf_op jit(solution)/shard_map/all_gather | solution.py:55
  7.9 167.3 %all-reduce.6.cloned.1.call-start = ((), (), s32[]{:S(2)}) async-start(), calls=%async_computation.3 | async-start | bytes 1572864 | tf_op jit(solution)/shard_map/psum | solution.py:60
  49.8 79.3 %copy-start.3 = (f32[6144]{0:T(1024)S(1)}, f32[6144]{0:T(1024)}, u32[]{:S(2)}) copy-start(f32[6144]{0:T(1024)} %param.14) | copy-start | bytes 73732
  97.8 232.1 %all-reduce.8.cloned.1.call-start = ((), (), s32[]{:S(2)}) async-start(), calls=%async_computation.4 | async-start | bytes 1572864 | tf_op jit(solution)/shard_map/psum | solution.py:84
  243.7 2.7 copy-start.1
  246.3 83.6 %copy-start.2 = (f32[512,384]{1,0:T(8,128)S(1)}, f32[512,384]{1,0:T(8,128)}, u32[]{:S(2)}) copy-start(f32[512,384]{1,0:T(8,128)} %all-reduce.6.cloned.1.call-done) | copy-start | bytes 2359300
  253.0 220.9 %all-reduce.10.cloned.1.call-start = ((), (), s32[]{:S(2)}) async-start(), calls=%async_computation.6 | async-start | bytes 1572864 | tf_op jit(solution)/shard_map/psum | solution.py:86
  334.3 227.6 %reduce-scatter.5.cloned.1.call-start = ((), (), s32[]{:S(2)}) async-start(), calls=%async_computation.7 | async-start | bytes 5013504 | tf_op jit(solution)/shard_map/reduce_scatter | solution.py:80
  342.1 324.8 %reduce-scatter.3.cloned.1.call-start = ((), (), s32[]{:S(2)}) async-start(), calls=%async_computation.5 | async-start | bytes 8912896 | tf_op jit(solution)/shard_map/reduce_scatter | solution.py:88
Sparse Core Ops, SparseCore 0:
  10.5 75.0 all-gather.1
  97.9 77.2 all-reduce.5
  253.2 76.7 all-reduce.7
  334.4 139.4 all-reduce.9
  477.9 83.9 reduce-scatter.4
  566.0 100.7 reduce-scatter.2
where the time goes:
time: 677 us; the launch traced here: 676 us
  waiting for transfers between devices  397 us (59%)
  blocking collectives  167 us (25%)
  matrix products  58.3 us (9%)
  other arithmetic  34.4 us (5%)
  between operations  14.2 us (2%)
    reduce_scatter x1, waiting for transfers between devices, on_device(): lax.psum_scatter(inner(tokens, dpre).astype(jnp.bfloat16), 'row', scatter...  103 us
    reduce_scatter x1, waiting for transfers between devices, on_device(): lax.psum_scatter(inner(student_n, grad_s).astype(jnp.bfloat16), 'row', sc...  85.6 us
    psum x1, waiting for transfers between devices, on_device(): dnorm = lax.psum(dnorm_part, 'proto')  76.8 us
    psum x1, blocking collectives, on_device(): loss = lax.psum(jnp.sum(weight * cross), ('row', 'proto'))  63.4 us
    psum x1, waiting for transfers between devices, on_device(): lax.psum(inner(hidden, dbott).astype(jnp.bfloat16), 'row')  57.5 us
    psum x1, blocking collectives, on_device(): counts = lax.psum(jnp.sum(onehot, axis=0), 'row')  38.4 us
    psum x1, waiting for transfers between devices, on_device(): bott = lax.psum(partial_value, 'proto')  37 us
    all_gather x1, waiting for transfers between devices, on_device(): lax.all_gather(w_in, 'row', axis=0, tiled=True)  35.8 us
  transfers between devices with their start and end apart: 6, of which 6 were waited for; matrix products, arithmetic and copies ran while one was open for 5% of the time, Pallas kernels for 0%

commit v1 on v0

--- a/solution.py
+++ b/solution.py
@@ -83,7 +83,9 @@
     dnorm_part = outer_last(grad_s, proto_student)
     dnorm = lax.psum(dnorm_part, "proto")
     dbott = back_norm(dnorm, recip, unit)
-    w_out_grad = lax.psum(inner(hidden, dbott).astype(jnp.bfloat16), "row").astype(jnp.float32)
+    w_out_grad = jnp.sum(
+        lax.all_gather(inner(hidden, dbott).astype(jnp.bfloat16), "row"), axis=0
+    ).astype(jnp.float32)
     dpre = (outer_last(dbott, w_out) * slope).astype(jnp.bfloat16)
     w_in_grad = lax.psum_scatter(
         inner(tokens, dpre).astype(jnp.bfloat16), "row", scatter_dimension=0, tiled=True

time: 677 us -> 630 us (0.931)
  waiting for transfers between devices: 397 us -> 335 us
  blocking collectives: 167 us -> 175 us
    all_gather x0 -> x1, waiting for transfers between devices: none -> 89.9 us  [on_device(): lax.all_gather(inner(hidden, dbott).astype(jnp.bfloat16), 'row')]
    reduce_scatter x1, waiting for transfers between devices: 85.6 us -> 0.01 us  [on_device(): lax.psum_scatter(inner(student_n, grad_s).astype(jnp.bfloat16), 'row', sc...]
    psum x1 -> x0, waiting for transfers between devices: 57.5 us -> none  [on_device(): lax.psum(inner(hidden, dbott).astype(jnp.bfloat16), 'row')]
    psum x1, blocking collectives: 63.4 us -> 71.4 us  [on_device(): loss = lax.psum(jnp.sum(weight * cross), ('row', 'proto'))]
    psum x1, waiting for transfers between devices: 76.8 us -> 69 us  [on_device(): dnorm = lax.psum(dnorm_part, 'proto')]
    reduce_sum x0 -> x1, other arithmetic: none -> 6.83 us  [on_device(): jnp.sum(lax.all_gather(inner(hidden, dbott).astype(jnp.bfloat16), 'row'),...]
  transfers between devices with their start and end apart: 6 -> 6, of which waited for: 6 -> 5; matrix products, arithmetic and copies ran while one was open for 5% -> 6% of each run, Pallas kernels for 0% -> 0%
where the time goes in v1:
time: 630 us; the launch traced here: 628 us
  waiting for transfers between devices  335 us (53%)
  blocking collectives  175 us (28%)
  matrix products  58.4 us (9%)
  other arithmetic  40.1 us (6%)
  between operations  14.2 us (2%)
    reduce_scatter x1, waiting for transfers between devices, on_device(): lax.psum_scatter(inner(tokens, dpre).astype(jnp.bfloat16), 'row', scatter...  103 us
    all_gather x1, waiting for transfers between devices, on_device(): lax.all_gather(inner(hidden, dbott).astype(jnp.bfloat16), 'row')  89.9 us
    psum x1, blocking collectives, on_device(): loss = lax.psum(jnp.sum(weight * cross), ('row', 'proto'))  71.4 us
    psum x1, waiting for transfers between devices, on_device(): dnorm = lax.psum(dnorm_part, 'proto')  69 us
    psum x1, blocking collectives, on_device(): counts = lax.psum(jnp.sum(onehot, axis=0), 'row')  38.4 us
    psum x1, waiting for transfers between devices, on_device(): bott = lax.psum(partial_value, 'proto')  36.8 us
    all_gather x1, waiting for transfers between devices, on_device(): lax.all_gather(w_in, 'row', axis=0, tiled=True)  35.8 us
    all_gather x1, blocking collectives, on_device(): lax.all_gather(teacher_norm(teacher_z), 'proto', axis=0, tiled=True)  31.3 us
  transfers between devices with their start and end apart: 6, of which 5 were waited for; matrix products, arithmetic and copies ran while one was open for 6% of the time, Pallas kernels for 0%

profile of v1, /device:TPU:0, one launch (start us, length us, event | category | flops | bytes accessed | tf_op | source)
XLA Modules:
  0.0 628.1 jit_solution(10057889930499249779)
XLA Ops:
  7.2 0.0 copy-start
  7.2 0.0 all-gather.4.cloned.1.call-start
  7.2 0.7 all-gather.4.cloned.1.call-update
  7.9 0.0 all-reduce.5.cloned.1.call-start
  8.0 0.8 convert_reduce_fusion
  8.8 38.4 %psum.42 = f32[64]{0:T(128)S(1)} all-reduce(f32[64]{0:T(128)S(1)} %convert_reduce_fusion), channel_id=1, replica_groups=mesh['row'=16,'proto'=8] {'row'}, use_global_device_ids=true, to_apply=%region_1.0 | all-reduce | flops 64 | bytes 512 | tf_op jit(solution)/shard_map/psum | solution.py:52
  47.2 0.9 fusion.9
  48.1 0.8 select_reduce_fusion
  48.9 0.9 fusion.10
  49.8 0.0 copy-start.3
  49.8 35.8 %all-gather.4.cloned.1.call-done = bf16[4096,1024]{1,0:T(8,128)(2,1)} async-done(((bf16[256,1024]{1,0:T(8,128)(2,1)}), bf16[4096,1024]{1,0:T(8,128)(2,1)}) %all-gather.4.cloned.1.call-update) | async-done | bytes 8388624 | tf_op jit(solution)/shard_map/all_gather | solution.py:55
  85.6 10.6 %multiply_convert_fusion.1 = (bf16[512,1024]{1,0:T(8,128)(2,1)S(1)}, f32[512,1024]{1,0:T(8,128)}) fusion(bf16[512,4096]{1,0:T(8,128)(2,1)} %param.8, bf16[4096,1024]{1,0:T(8,128)(2,1)} %all-gather.4.cloned.1.call-done), kind=kOutput, calls=%fused_computation.19 | convolution fusion | flops 4297588736 | bytes 15728640 | tf_op jit(solution)/shard_map/dot_general | solution.py:54
  96.2 1.6 fusion.14
  97.7 0.0 all-reduce.5.cloned.1.call-update
  97.8 0.0 all-reduce.7.cloned.1.call-start
  97.8 31.3 %all_gather.12 = bf16[512,384]{1,0:T(8,128)(2,1)S(1)} all-gather(bf16[64,384]{1,0:T(8,128)(2,1)S(1)} %fusion.10), channel_id=1, replica_groups=mesh['row'=16,'proto'=8] {'proto'}, dimensions={0}, use_global_device_ids=true | all-gather | bytes 442368 | tf_op jit(solution)/shard_map/all_gather | solution.py:63
  129.1 9.1 %fusion = (f32[512]{0:T(512)S(1)}, f32[512,6144]{1,0:T(8,128)}) fusion(f32[6144]{0:T(1024)S(1)} %copy-done.3, bf16[512,384]{1,0:T(8,128)(2,1)S(1)} %all_gather.12, bf16[384,6144]{1,0:T(8,128)(2,1)} %param.13), kind=kOutput, calls=%fused_computation.7 | convolution fusion | flops 2425355776 | bytes 17721344 | tf_op jit(solution)/shard_map/dot_general | solution.py:65
  138.2 36.8 %all-reduce.5.cloned.1.call-done = f32[512,384]{1,0:T(8,128)} async-done(((f32[512,384]{1,0:T(8,128)}), f32[512,384]{1,0:T(8,128)}) %all-reduce.5.cloned.1.call-update) | async-done | bytes 786448 | tf_op jit(solution)/shard_map/psum | solution.py:60
  175.0 1.3 multiply_reduce_fusion.3
  176.3 10.7 %multiply_reduce_fusion.1 = (f32[512]{0:T(512)S(1)}, f32[512,6144]{1,0:T(8,128)}) fusion(bf16[384,6144]{1,0:T(8,128)(2,1)} %param.12, f32[512,384]{1,0:T(8,128)} %all-reduce.5.cloned.1.call-done, f32[512]{0:T(512)S(1)} %add_rsqrt_fusion), kind=kOutput, calls=%fused_computation.6 | convolution fusion | flops 2422603264 | bytes 18092032 | tf_op jit(solution)/shard_map/dot_general | solution.py:67
  186.9 17.9 %all-reduce.1 = (f32[512]{0:T(512)S(1)}, f32[512]{0:T(512)S(1)}) all-reduce(f32[512]{0:T(512)S(1)} %get-tuple-element.20, f32[512]{0:T(512)S(1)} %get-tuple-element.22), channel_id=1, replica_groups=mesh['row'=16,'proto'=8] {'proto'}, use_global_device_ids=true, to_apply=%region_11.0 | all-reduce | flops 1024 | bytes 8192 | tf_op jit(solution)/shard_map/pmax | solution.py:70
  204.8 10.3 %exponential_reduce_fusion = (f32[512]{0:T(512)S(1)}, f32[512]{0:T(512)S(1)}) fusion(f32[512,6144]{1,0:T(8,128)} %get-tuple-element.21, f32[512]{0:T(512)S(1)} %get-tuple-element.14, f32[512]{0:T(512)S(1)} %get-tuple-element.15, f32[512,6144]{1,0:T(8,128)} %get-tuple-element.23, f32[6144]{0:T(1024)S(1)} %copy-done.3), kind=kLoop, calls=%fused_computation.4 | loop fusion | flops 22019072 | bytes 25198592 | tf_op jit(solution)/shard_map/reduce_sum | solution.py:73
  215.1 16.4 %all-reduce = (f32[512]{0:T(512)S(1)}, f32[512]{0:T(512)S(1)}) all-reduce(f32[512]{0:T(512)S(1)} %get-tuple-element.24, f32[512]{0:T(512)S(1)} %get-tuple-element.25), channel_id=1, replica_groups=mesh['row'=16,'proto'=8] {'proto'}, use_global_device_ids=true, to_apply=%region_13.0 | all-reduce | flops 1024 | bytes 8192 | tf_op jit(solution)/shard_map/psum | solution.py:73
  231.5 12.0 %multiply_convert_fusion = (bf16[512,6144]{1,0:T(8,128)(2,1)S(1)}, f32[512]{0:T(512)S(1)}) fusion(f32[512,6144]{1,0:T(8,128)} %get-tuple-element.21, f32[512]{0:T(512)S(1)} %get-tuple-element.12, f32[512]{0:T(512)S(1)} %broadcast_multiply_fusion, f32[512]{0:T(512)S(1)} %get-tuple-element.14, f32[512]{0:T(512)S(1)} %get-tuple-element.13, ...), kind=kLoop, calls=%fused_computation | loop fusion | flops 44039680 | bytes 31496192 | tf_op jit(solution)/shard_map/convert_element_type | solution.py:79
  243.4 0.0 copy-start.1
  243.5 2.7 copy-done.1
  246.2 6.7 %fusion.15 = f32[512,384]{1,0:T(8,128)} fusion(bf16[512,6144]{1,0:T(8,128)(2,1)S(1)} %get-tuple-element.16, bf16[384,6144]{1,0:T(8,128)(2,1)} %param.12), kind=kOutput, calls=%fused_computation.42 | convolution fusion | flops 2415919104 | bytes 11796480 | tf_op jit(solution)/shard_map/dot_general | solution.py:25
  252.9 0.0 all-reduce.7.cloned.1.call-update
  252.9 0.0 reduce-scatter.5.cloned.1.call-start
  253.0 7.7 %convolution_convert_fusion = bf16[384,6144]{1,0:T(8,128)(2,1)} fusion(bf16[512,6144]{1,0:T(8,128)(2,1)} %copy-done.1, f32[512,384]{1,0:T(8,128)S(1)} %copy-done.2, f32[512]{0:T(512)S(1)} %add_rsqrt_fusion), kind=kOutput, calls=%fused_computation.10 | convolution fusion | flops 2418671616 | bytes 11798528 | tf_op jit(solution)/shard_map/dot_general | solution.py:19
  260.6 0.0 reduce-scatter.5.cloned.1.call-update
  260.7 0.0 reduce-scatter.3.cloned.1.call-start
  260.7 69.0 %all-reduce.7.cloned.1.call-done = f32[512,384]{1,0:T(8,128)} async-done(((f32[512,384]{1,0:T(8,128)}), f32[512,384]{1,0:T(8,128)}) %all-reduce.7.cloned.1.call-update) | async-done | bytes 786448 | tf_op jit(solution)/shard_map/psum | solution.py:84
  329.8 1.4 multiply_reduce_fusion.2
  331.1 1.3 multiply_convert_fusion.2
  332.5 10.4 %convert_bitcast_fusion = bf16[4096,1024]{0,1:T(8,128)(2,1)} fusion(bf16[512,4096]{1,0:T(8,128)(2,1)} %param.8, f32[512,1024]{1,0:T(8,128)} %get-tuple-element.19, bf16[512,384]{1,0:T(8,128)(2,1)S(1)} %multiply_convert_fusion.2, bf16[1024,384]{1,0:T(8,128)(2,1)S(1)} %copy-done), kind=kOutput, calls=%fused_computation.11 | convolution fusion | flops 4707057664 | bytes 15859712 | tf_op jit(solution)/shard_map/dot_general | solution.py:19
  342.9 0.0 reduce-scatter.3.cloned.1.call-update
  343.0 0.0 all-gather.6.cloned.1.call-start
  343.0 1.7 convolution_convert_fusion.1
  344.7 0.0 all-gather.6.cloned.1.call-update
  344.7 0.6 multiply_reduce_fusion.4
  345.3 71.4 %psum.46 = f32[]{:T(128)} all-reduce(f32[]{:T(128)} %multiply_reduce_fusion.4), channel_id=1, replica_groups=mesh['row'=16,'proto'=8] {'row','proto'}, use_global_device_ids=true, to_apply=%region_16.0 | all-reduce | flops 1 | bytes 8 | tf_op jit(solution)/shard_map/psum | solution.py:78
  416.7 1.8 convert_element_type.61
  418.5 102.6 %reduce-scatter.3.cloned.1.call-done = bf16[256,1024]{0,1:T(8,128)(2,1)} async-done(((bf16[4096,1024]{0,1:T(8,128)(2,1)}), bf16[256,1024]{0,1:T(8,128)(2,1)}) %reduce-scatter.3.cloned.1.call-update) | async-done | bytes 524304 | tf_op jit(solution)/shard_map/reduce_scatter | solution.py:90
  521.1 2.2 copy.13
  523.3 89.9 %all-gather.6.cloned.1.call-done = bf16[16384,384]{1,0:T(8,128)(2,1)} async-done(((bf16[1024,384]{1,0:T(8,128)(2,1)}), bf16[16384,384]{1,0:T(8,128)(2,1)}) %all-gather.6.cloned.1.call-update) | async-done | bytes 12582928 | tf_op jit(solution)/shard_map/all_gather | solution.py:87
  613.2 6.8 %reduce_sum.102 = bf16[1024,384]{1,0:T(8,128)(2,1)S(1)} reduce(bf16[16,1024,384]{2,1,0:T(8,128)(2,1)} %bitcast.18, bf16[]{:T(256)} %constant.31.clone.1), dimensions={0}, to_apply=%region_20.0 | reduce | flops 5898240 | bytes 13369346 | tf_op jit(solution)/shard_map/reduce_sum | solution.py:86
  620.0 1.2 convert_element_type.59
  (9 shorter events, 0.0 us)
Async XLA Ops:
  7.2 89.0 %copy-start = (bf16[1024,384]{1,0:T(8,128)(2,1)S(1)}, bf16[1024,384]{1,0:T(8,128)(2,1)}, u32[]{:S(2)}) copy-start(bf16[1024,384]{1,0:T(8,128)(2,1)} %param.10) | copy-start | bytes 2359300
  7.2 78.4 %all-gather.4.cloned.1.call-start = ((), (), s32[]{:S(2)}) async-start(), calls=%async_computation.2 | async-start | bytes 8912896 | tf_op jit(solution)/shard_map/all_gather | solution.py:55
  7.9 167.1 %all-reduce.5.cloned.1.call-start = ((), (), s32[]{:S(2)}) async-start(), calls=%async_computation.3 | async-start | bytes 1572864 | tf_op jit(solution)/shard_map/psum | solution.py:60
  49.8 79.3 %copy-start.3 = (f32[6144]{0:T(1024)S(1)}, f32[6144]{0:T(1024)}, u32[]{:S(2)}) copy-start(f32[6144]{0:T(1024)} %param.14) | copy-start | bytes 73732
  97.8 232.0 %all-reduce.7.cloned.1.call-start = ((), (), s32[]{:S(2)}) async-start(), calls=%async_computation.4 | async-start | bytes 1572864 | tf_op jit(solution)/shard_map/psum | solution.py:84
  243.4 2.7 copy-start.1
  246.2 6.8 %copy-start.2 = (f32[512,384]{1,0:T(8,128)S(1)}, f32[512,384]{1,0:T(8,128)}, u32[]{:S(2)}) copy-start(f32[512,384]{1,0:T(8,128)} %all-reduce.5.cloned.1.call-done) | copy-start | bytes 2359300
  252.9 163.8 %reduce-scatter.5.cloned.1.call-start = ((), (), s32[]{:S(2)}) async-start(), calls=%async_computation.6 | async-start | bytes 5013504 | tf_op jit(solution)/shard_map/reduce_scatter | solution.py:80
  260.7 260.5 %reduce-scatter.3.cloned.1.call-start = ((), (), s32[]{:S(2)}) async-start(), calls=%async_computation.5 | async-start | bytes 8912896 | tf_op jit(solution)/shard_map/reduce_scatter | solution.py:90
  343.0 270.2 %all-gather.6.cloned.1.call-start = ((), (), s32[]{:S(2)}) async-start(), calls=%async_computation.7 | async-start | bytes 13369344 | tf_op jit(solution)/shard_map/all_gather | solution.py:87
Sparse Core Ops, SparseCore 0:
  10.5 75.0 all-gather.3
  97.9 77.0 all-reduce.4
  253.0 76.7 all-reduce.6
  333.7 82.4 reduce-scatter.4
  420.3 100.7 reduce-scatter.2
  524.0 89.1 all-gather.5
